TPU v7x, 256 devices: a whole 4x4x8 slice. The times are simulated.
256 devices in a mesh: bench: 32 (over x, y, core), sweep: 8 (over z).
Axes of the slice: x: 4, y: 4, z: 8, core: 2. Of those that a mesh axis runs over, the one named last changes fastest.
Arguments:
- finished: bfloat16 [1024, 8, 64, 128], P('bench', 'sweep'), may hold values from -6 to 6
- noise: bfloat16 [1024, 8, 64, 128], P('bench', 'sweep'), may hold values from -6 to 6
- factors: bfloat16 [1024, 8, 8, 128, 128], P('bench', 'sweep'), may hold values from -0.1875 to 0.1875
- chol: bfloat16 [1024, 8, 128, 128], P('bench', 'sweep'), may hold values from -0.1875 to 0.1875
- front_w: bfloat16 [1024, 8, 128, 128], P('bench', 'sweep'), may hold values from -0.5 to 0.5
- parents: int32 [1024, 8, 8], P('bench', 'sweep'), may hold values from 0 to 1023, as said below
Outputs:
- evolved: float32 [1024, 8, 64, 128], P('bench', 'sweep')
Inputs may be any that keep to these rules, and one draw needn't show every extreme that they name: A parent row p lies on the bench owner p // 32. The 256 parents of the tiles of one bench group and sweep column name at most 16 rows of one owner, exactly 16 for some owner, and lie on at most 17 owners.
All inputs are finite; a program needn't handle non-finite values.
Results may differ from a plain program's by a relative error of at most 0.0003.
Values may be sent and summed in bfloat16 or wider, within the bound.
No kernel may reach another device: no remote copies, remote signals or barrier semaphores. Data moves between devices by JAX's collectives and lax.ppermute only.
A program may use at most 128 MiB of HBM per device.

v0:
```python
import jax
import jax.numpy as jnp
from jax import lax
from jax.sharding import PartitionSpec as P


def from_behind(array, axis, by):
    size = lax.axis_size(axis)
    pairs = [(i, i + by) for i in range(size) if 0 <= i + by < size]
    return lax.ppermute(array, axis, pairs)


def body(finished, noise, factors, chol, front_w, parents):
    pool_local = finished[:, 0]
    tile_count = noise.shape[0]
    fan = parents.shape[2]
    wanted = parents[:, 0].reshape(-1)
    whole_pool = lax.all_gather(finished, "bench", axis=0, tiled=True)
    chosen = jnp.take(whole_pool[:, 0], wanted, axis=0)
    chosen = chosen.reshape((tile_count, fan) + pool_local.shape[1:])
    local = jnp.einsum("jkrm,jkmn->jrn", chosen, factors[:, 0], preferred_element_type=jnp.float32)
    local = local + jnp.einsum(
        "jrm,jmn->jrn", noise[:, 0], chol[:, 0], preferred_element_type=jnp.float32
    )
    weights = front_w[:, 0].astype(jnp.float32)
    last_weight = weights[tile_count - 1]
    last_local = local[tile_count - 1]
    incoming = jnp.zeros_like(last_local)
    outgoing = last_local
    for step in range(lax.axis_size("sweep") - 1):
        incoming = from_behind(outgoing, "sweep", 1)
        outgoing = last_local + jnp.dot(incoming, last_weight, precision=lax.Precision.HIGHEST)
    tiles = local + jnp.einsum("rm,jmn->jrn", incoming, weights, precision=lax.Precision.HIGHEST)
    return tiles[:, None]


def solution(mesh):
    return jax.shard_map(
        body,
        mesh=mesh,
        in_specs=(
            P("bench", "sweep", None, None),
            P("bench", "sweep", None, None),
            P("bench", "sweep", None, None, None),
            P("bench", "sweep", None, None),
            P("bench", "sweep", None, None),
            P("bench", "sweep", None),
        ),
        out_specs=P("bench", "sweep", None, None),
        check_vma=False,
    )
```

profile of v0, /device:TPU:128, one launch (start us, length us, event | category | flops | bytes accessed | tf_op | source)
XLA Modules:
  0.0 163.4 jit_solution(4601643470623711922)
XLA Ops:
  6.5 0.0 copy-start
  6.5 0.0 all-gather.2.cloned.1.call-start
  6.5 0.7 all-gather.2.cloned.1.call-update
  7.3 0.8 copy.13
  8.0 0.1 reshape_squeeze.6
  8.1 0.7 compare_and_fusion
  8.8 0.1 copy.12
  8.9 80.1 %all-gather.2.cloned.1.call-done = bf16[1024,1,64,128]{3,2,1,0:T(8,128)(2,1)} async-done(((bf16[32,1,64,128]{3,2,1,0:T(8,128)(2,1)}), bf16[1024,1,64,128]{3,2,1,0:T(8,128)(2,1)}) %all-gather.2.cloned.1.call-update) | async-done | bytes 16777232 | tf_op jit(solution)/shard_map/all_gather | solution.py:18
  89.0 8.8 %gather_fusion = bf16[256,64,128]{2,1,0:T(8,128)(2,1)} fusion(bf16[1024,64,128]{2,1,0:T(8,128)(2,1)} %bitcast.73, s32[1024]{0:T(1024)S(1)} %pad_clamp_fusion), kind=kCustom, calls=%fused_computation | custom fusion | bytes 8389632 | tf_op jit(solution)/shard_map/jit(_take)/gather | solution.py:19
  97.8 0.0 copy-start.2
  97.8 0.0 copy-start.1
  97.8 6.6 %fusion.7 = f32[32,64,128]{2,1,0:T(8,128)S(1)} fusion(bf16[32,1,8,128,128]{4,3,2,1,0:T(8,128)(2,1)} %param.8, bf16[32,8,64,128]{3,2,1,0:T(8,128)(2,1)} %bitcast.72, pred[32,8]{1,0:T(8,128)(4,1)S(1)} %copy.12), kind=kOutput, calls=%fused_computation.10 | convolution fusion | flops 538968064 | bytes 13631744 | tf_op jit(solution)/shard_map/jkrm,jkmn->jrn/dot_general | solution.py:21
  104.4 0.0 copy-done
  104.4 0.0 copy-done.2
  104.4 0.4 convolution_add_fusion
  104.9 2.6 %collective-permute-start = (f32[64,128]{1,0:T(8,128)S(1)}, f32[64,128]{1,0:T(8,128)S(1)}, u32[]{:S(2)}, u32[]{:S(2)}) collective-permute-start(f32[64,128]{1,0:T(8,128)S(1)} %slice_bitcast_fusion), channel_id=1, source_target_pairs={{0,1},{1,2},{2,3},{3,4},{4,5},{5,6},{6,7},{8,9},{9,10},{10,11},{11... | collective-permute-start | bytes 98312 | tf_op jit(solution)/shard_map/ppermute | solution.py:10
  107.5 4.4 %collective-permute-done = f32[64,128]{1,0:T(8,128)S(1)} collective-permute-done((f32[64,128]{1,0:T(8,128)S(1)}, f32[64,128]{1,0:T(8,128)S(1)}, u32[]{:S(2)}, u32[]{:S(2)}) %collective-permute-start) | collective-permute-done | bytes 32800 | tf_op jit(solution)/shard_map/ppermute | solution.py:10
  111.9 0.0 copy-done.1
  111.9 0.2 convolution_add_fusion.6
  112.1 1.9 %collective-permute-start.1 = (f32[64,128]{1,0:T(8,128)S(1)}, f32[64,128]{1,0:T(8,128)S(1)}, u32[]{:S(2)}, u32[]{:S(2)}) collective-permute-start(f32[64,128]{1,0:T(8,128)S(1)} %convolution_add_fusion.6), channel_id=1, source_target_pairs={{0,1},{1,2},{2,3},{3,4},{4,5},{5,6},{6,7},{8,9},{9,10},{10,11},{11... | collective-permute-start | bytes 98312 | tf_op jit(solution)/shard_map/ppermute | solution.py:10
  114.0 5.1 %collective-permute-done.1 = f32[64,128]{1,0:T(8,128)S(1)} collective-permute-done((f32[64,128]{1,0:T(8,128)S(1)}, f32[64,128]{1,0:T(8,128)S(1)}, u32[]{:S(2)}, u32[]{:S(2)}) %collective-permute-start.1) | collective-permute-done | bytes 32800 | tf_op jit(solution)/shard_map/ppermute | solution.py:10
  119.1 0.2 convolution_add_fusion.5
  119.3 1.9 %collective-permute-start.2 = (f32[64,128]{1,0:T(8,128)S(1)}, f32[64,128]{1,0:T(8,128)S(1)}, u32[]{:S(2)}, u32[]{:S(2)}) collective-permute-start(f32[64,128]{1,0:T(8,128)S(1)} %convolution_add_fusion.5), channel_id=1, source_target_pairs={{0,1},{1,2},{2,3},{3,4},{4,5},{5,6},{6,7},{8,9},{9,10},{10,11},{11... | collective-permute-start | bytes 98312 | tf_op jit(solution)/shard_map/ppermute | solution.py:10
  121.2 5.1 %collective-permute-done.2 = f32[64,128]{1,0:T(8,128)S(1)} collective-permute-done((f32[64,128]{1,0:T(8,128)S(1)}, f32[64,128]{1,0:T(8,128)S(1)}, u32[]{:S(2)}, u32[]{:S(2)}) %collective-permute-start.2) | collective-permute-done | bytes 32800 | tf_op jit(solution)/shard_map/ppermute | solution.py:10
  126.3 0.2 convolution_add_fusion.4
  126.5 1.9 %collective-permute-start.3 = (f32[64,128]{1,0:T(8,128)S(1)}, f32[64,128]{1,0:T(8,128)S(1)}, u32[]{:S(2)}, u32[]{:S(2)}) collective-permute-start(f32[64,128]{1,0:T(8,128)S(1)} %convolution_add_fusion.4), channel_id=1, source_target_pairs={{0,1},{1,2},{2,3},{3,4},{4,5},{5,6},{6,7},{8,9},{9,10},{10,11},{11... | collective-permute-start | bytes 98312 | tf_op jit(solution)/shard_map/ppermute | solution.py:10
  128.4 5.1 %collective-permute-done.3 = f32[64,128]{1,0:T(8,128)S(1)} collective-permute-done((f32[64,128]{1,0:T(8,128)S(1)}, f32[64,128]{1,0:T(8,128)S(1)}, u32[]{:S(2)}, u32[]{:S(2)}) %collective-permute-start.3) | collective-permute-done | bytes 32800 | tf_op jit(solution)/shard_map/ppermute | solution.py:10
  133.5 0.2 convolution_add_fusion.3
  133.6 1.9 %collective-permute-start.4 = (f32[64,128]{1,0:T(8,128)S(1)}, f32[64,128]{1,0:T(8,128)S(1)}, u32[]{:S(2)}, u32[]{:S(2)}) collective-permute-start(f32[64,128]{1,0:T(8,128)S(1)} %convolution_add_fusion.3), channel_id=1, source_target_pairs={{0,1},{1,2},{2,3},{3,4},{4,5},{5,6},{6,7},{8,9},{9,10},{10,11},{11... | collective-permute-start | bytes 98312 | tf_op jit(solution)/shard_map/ppermute | solution.py:10
  135.6 5.1 %collective-permute-done.4 = f32[64,128]{1,0:T(8,128)S(1)} collective-permute-done((f32[64,128]{1,0:T(8,128)S(1)}, f32[64,128]{1,0:T(8,128)S(1)}, u32[]{:S(2)}, u32[]{:S(2)}) %collective-permute-start.4) | collective-permute-done | bytes 32800 | tf_op jit(solution)/shard_map/ppermute | solution.py:10
  140.7 0.2 convolution_add_fusion.2
  140.8 1.9 %collective-permute-start.5 = (f32[64,128]{1,0:T(8,128)S(1)}, f32[64,128]{1,0:T(8,128)S(1)}, u32[]{:S(2)}, u32[]{:S(2)}) collective-permute-start(f32[64,128]{1,0:T(8,128)S(1)} %convolution_add_fusion.2), channel_id=1, source_target_pairs={{0,1},{1,2},{2,3},{3,4},{4,5},{5,6},{6,7},{8,9},{9,10},{10,11},{11... | collective-permute-start | bytes 98312 | tf_op jit(solution)/shard_map/ppermute | solution.py:10
  142.8 5.1 %collective-permute-done.5 = f32[64,128]{1,0:T(8,128)S(1)} collective-permute-done((f32[64,128]{1,0:T(8,128)S(1)}, f32[64,128]{1,0:T(8,128)S(1)}, u32[]{:S(2)}, u32[]{:S(2)}) %collective-permute-start.5) | collective-permute-done | bytes 32800 | tf_op jit(solution)/shard_map/ppermute | solution.py:10
  147.9 0.2 convolution_add_fusion.1
  148.0 1.9 %collective-permute-start.6 = (f32[64,128]{1,0:T(8,128)S(1)}, f32[64,128]{1,0:T(8,128)S(1)}, u32[]{:S(2)}, u32[]{:S(2)}) collective-permute-start(f32[64,128]{1,0:T(8,128)S(1)} %convolution_add_fusion.1), channel_id=1, source_target_pairs={{0,1},{1,2},{2,3},{3,4},{4,5},{5,6},{6,7},{8,9},{9,10},{10,11},{11... | collective-permute-start | bytes 98312 | tf_op jit(solution)/shard_map/ppermute | solution.py:10
  150.0 5.1 %collective-permute-done.6 = f32[64,128]{1,0:T(8,128)S(1)} collective-permute-done((f32[64,128]{1,0:T(8,128)S(1)}, f32[64,128]{1,0:T(8,128)S(1)}, u32[]{:S(2)}, u32[]{:S(2)}) %collective-permute-start.6) | collective-permute-done | bytes 32800 | tf_op jit(solution)/shard_map/ppermute | solution.py:10
  155.0 1.5 fusion.6
  (3 shorter events, 0.0 us)
Async XLA Ops:
  6.5 97.9 %copy-start = (bf16[32,1,128,128]{3,2,1,0:T(8,128)(2,1)S(1)}, bf16[32,1,128,128]{3,2,1,0:T(8,128)(2,1)}, u32[]{:S(2)}) copy-start(bf16[32,1,128,128]{3,2,1,0:T(8,128)(2,1)} %param.9) | copy-start | bytes 3145732
  6.5 82.4 %all-gather.2.cloned.1.call-start = ((), (), s32[]{:S(2)}) async-start(), calls=%async_computation | async-start | bytes 17301504 | tf_op jit(solution)/shard_map/all_gather | solution.py:18
  97.8 6.6 %copy-start.2 = (bf16[32,1,64,128]{3,2,1,0:T(8,128)(2,1)S(1)}, bf16[32,1,64,128]{3,2,1,0:T(8,128)(2,1)}, u32[]{:S(2)}) copy-start(bf16[32,1,64,128]{3,2,1,0:T(8,128)(2,1)} %param.7) | copy-start | bytes 1572868
  97.8 14.1 %copy-start.1 = (bf16[32,1,128,128]{3,2,1,0:T(8,128)(2,1)S(1)}, bf16[32,1,128,128]{3,2,1,0:T(8,128)(2,1)}, u32[]{:S(2)}) copy-start(bf16[32,1,128,128]{3,2,1,0:T(8,128)(2,1)} %param.10) | copy-start | bytes 3145732
  104.9 7.0 %collective-permute-start = (f32[64,128]{1,0:T(8,128)S(1)}, f32[64,128]{1,0:T(8,128)S(1)}, u32[]{:S(2)}, u32[]{:S(2)}) collective-permute-start(f32[64,128]{1,0:T(8,128)S(1)} %slice_bitcast_fusion), channel_id=1, source_target_pairs={{0,1},{1,2},{2,3},{3,4},{4,5},{5,6},{6,7},{8,9},{9,10},{10,11},{11... | collective-permute-start | bytes 98312 | tf_op jit(solution)/shard_map/ppermute | solution.py:10
  112.1 7.0 %collective-permute-start.1 = (f32[64,128]{1,0:T(8,128)S(1)}, f32[64,128]{1,0:T(8,128)S(1)}, u32[]{:S(2)}, u32[]{:S(2)}) collective-permute-start(f32[64,128]{1,0:T(8,128)S(1)} %convolution_add_fusion.6), channel_id=1, source_target_pairs={{0,1},{1,2},{2,3},{3,4},{4,5},{5,6},{6,7},{8,9},{9,10},{10,11},{11... | collective-permute-start | bytes 98312 | tf_op jit(solution)/shard_map/ppermute | solution.py:10
  119.3 7.0 %collective-permute-start.2 = (f32[64,128]{1,0:T(8,128)S(1)}, f32[64,128]{1,0:T(8,128)S(1)}, u32[]{:S(2)}, u32[]{:S(2)}) collective-permute-start(f32[64,128]{1,0:T(8,128)S(1)} %convolution_add_fusion.5), channel_id=1, source_target_pairs={{0,1},{1,2},{2,3},{3,4},{4,5},{5,6},{6,7},{8,9},{9,10},{10,11},{11... | collective-permute-start | bytes 98312 | tf_op jit(solution)/shard_map/ppermute | solution.py:10
  126.5 7.0 %collective-permute-start.3 = (f32[64,128]{1,0:T(8,128)S(1)}, f32[64,128]{1,0:T(8,128)S(1)}, u32[]{:S(2)}, u32[]{:S(2)}) collective-permute-start(f32[64,128]{1,0:T(8,128)S(1)} %convolution_add_fusion.4), channel_id=1, source_target_pairs={{0,1},{1,2},{2,3},{3,4},{4,5},{5,6},{6,7},{8,9},{9,10},{10,11},{11... | collective-permute-start | bytes 98312 | tf_op jit(solution)/shard_map/ppermute | solution.py:10
  133.6 7.0 %collective-permute-start.4 = (f32[64,128]{1,0:T(8,128)S(1)}, f32[64,128]{1,0:T(8,128)S(1)}, u32[]{:S(2)}, u32[]{:S(2)}) collective-permute-start(f32[64,128]{1,0:T(8,128)S(1)} %convolution_add_fusion.3), channel_id=1, source_target_pairs={{0,1},{1,2},{2,3},{3,4},{4,5},{5,6},{6,7},{8,9},{9,10},{10,11},{11... | collective-permute-start | bytes 98312 | tf_op jit(solution)/shard_map/ppermute | solution.py:10
  140.8 7.0 %collective-permute-start.5 = (f32[64,128]{1,0:T(8,128)S(1)}, f32[64,128]{1,0:T(8,128)S(1)}, u32[]{:S(2)}, u32[]{:S(2)}) collective-permute-start(f32[64,128]{1,0:T(8,128)S(1)} %convolution_add_fusion.2), channel_id=1, source_target_pairs={{0,1},{1,2},{2,3},{3,4},{4,5},{5,6},{6,7},{8,9},{9,10},{10,11},{11... | collective-permute-start | bytes 98312 | tf_op jit(solution)/shard_map/ppermute | solution.py:10
  148.0 7.0 %collective-permute-start.6 = (f32[64,128]{1,0:T(8,128)S(1)}, f32[64,128]{1,0:T(8,128)S(1)}, u32[]{:S(2)}, u32[]{:S(2)}) collective-permute-start(f32[64,128]{1,0:T(8,128)S(1)} %convolution_add_fusion.1), channel_id=1, source_target_pairs={{0,1},{1,2},{2,3},{3,4},{4,5},{5,6},{6,7},{8,9},{9,10},{10,11},{11... | collective-permute-start | bytes 98312 | tf_op jit(solution)/shard_map/ppermute | solution.py:10
Sparse Core Ops, SparseCore 0:
  9.9 79.0 all-gather.1
where the time goes:
time: 164 us; the launch traced here: 163 us
  waiting for transfers between devices  116 us (71%)
  starting transfers between devices  14.1 us (9%)
  between operations  13.5 us (8%)
  local copies, waits for them, and re-layouts  9.77 us (6%)
  matrix products  9.56 us (6%)
    all_gather x1, waiting for transfers between devices, body(): whole_pool = lax.all_gather(finished, 'bench', axis=0, tiled=True)  80.1 us
    ppermute x7, waiting for transfers between devices, from_behind(): return lax.ppermute(array, axis, pairs)  35 us
    ppermute x7, starting transfers between devices, from_behind(): return lax.ppermute(array, axis, pairs)  14.1 us
    gather x1, local copies, waits for them, and re-layouts, body(): chosen = jnp.take(whole_pool[:, 0], wanted, axis=0)  8.8 us
    dot_general x1, matrix products, body(): jnp.einsum('jkrm,jkmn->jrn', chosen, factors[:, 0], preferred_element_typ...  6.61 us
  transfers between devices with their start and end apart: 8, of which 8 were waited for; matrix products, arithmetic and copies ran while one was open for 1% of the time, Pallas kernels for 0%

commit v1 on v0

--- a/solution.py
+++ b/solution.py
@@ -2,6 +2,19 @@
 import jax.numpy as jnp
 from jax import lax
 from jax.sharding import PartitionSpec as P
+
+
+def load_run(v0, group_axis):
+    arr_now = jnp.concatenate(
+        lax.all_to_all(
+            jnp.stack([v0] * lax.axis_size(group_axis), axis=0),
+            axis_name=group_axis,
+            concat_axis=0,
+            split_axis=0,
+        ),
+        0,
+    )
+    return arr_now
 
 
 def from_behind(array, axis, by):
@@ -15,7 +28,7 @@
     tile_count = noise.shape[0]
     fan = parents.shape[2]
     wanted = parents[:, 0].reshape(-1)
-    whole_pool = lax.all_gather(finished, "bench", axis=0, tiled=True)
+    whole_pool = load_run(finished, "bench")
     chosen = jnp.take(whole_pool[:, 0], wanted, axis=0)
     chosen = chosen.reshape((tile_count, fan) + pool_local.shape[1:])
     local = jnp.einsum("jkrm,jkmn->jrn", chosen, factors[:, 0], preferred_element_type=jnp.float32)

time: 164 us -> 352 us (2.15)
  the two profiles are of different devices: /device:TPU:128 before, /device:TPU:140 now
where the time goes in v1:
time: 352 us
  waiting for transfers between devices  304 us (86%)
  starting transfers between devices  22.1 us (6%)
  local copies, waits for them, and re-layouts  16.2 us (5%)
  matrix products  9.56 us (3%)
    all_to_all x1, waiting for transfers between devices, load_run(): lax.all_to_all(jnp.stack([v0] * lax.axis_size(group_axis), axis=0), axis_...  269 us
    ppermute x7, waiting for transfers between devices, from_behind(): return lax.ppermute(array, axis, pairs)  35 us
    ppermute x7, starting transfers between devices, from_behind(): return lax.ppermute(array, axis, pairs)  14.4 us
    gather x1, local copies, waits for them, and re-layouts, body(): chosen = jnp.take(whole_pool[:, 0], wanted, axis=0)  8.8 us
    all_to_all x1, starting transfers between devices, load_run(): lax.all_to_all(jnp.stack([v0] * lax.axis_size(group_axis), axis=0), axis_...  7.67 us
    another operation x1, local copies, waits for them, and re-layouts, load_run(): jnp.stack([v0] * lax.axis_size(group_axis), axis=0)  7.14 us
  transfers between devices with their start and end apart: 8, of which 8 were waited for; matrix products, arithmetic and copies ran while one was open for 0% of the time, Pallas kernels for 0%

profile of v1, /device:TPU:140, one launch (start us, length us, event | category | flops | bytes accessed | tf_op | source)
XLA Modules:
  0.0 351.8 jit_solution(536660489840830058)
XLA Ops:
  0.0 0.0 copy-start
  0.0 7.1 %stack.2 = bf16[32,32,1,64,128]{4,3,2,1,0:T(8,128)(2,1)} broadcast(bf16[32,64,128]{2,1,0:T(8,128)(2,1)} %bitcast.74), dimensions={1,3,4} | broadcast | bytes 17301504 | tf_op jit(solution)/shard_map/stack | solution.py:10
  7.1 0.0 copy-start.3
  7.1 7.7 %all-to-all-start = ((bf16[32,32,1,64,128]{4,3,2,1,0:T(8,128)(2,1)}), bf16[32,32,1,64,128]{4,3,2,1,0:T(8,128)(2,1)}, u32[]{:S(2)}, u32[]{:S(2)}) async-start(bf16[32,32,1,64,128]{4,3,2,1,0:T(8,128)(2,1)} %stack.2), calls=%async_computation | async-start | bytes 33554432 | tf_op jit(solution)/shard_map/all_to_all | solution.py:9
  14.8 0.0 copy-done.3
  14.8 0.1 copy.10
  14.9 0.1 reshape_squeeze.6
  15.0 0.1 copy.9
  15.1 268.7 %all-to-all-done = bf16[32,32,1,64,128]{4,3,2,1,0:T(8,128)(2,1)} async-done(((bf16[32,32,1,64,128]{4,3,2,1,0:T(8,128)(2,1)}), bf16[32,32,1,64,128]{4,3,2,1,0:T(8,128)(2,1)}, u32[]{:S(2)}, u32[]{:S(2)}) %all-to-all-start) | async-done | bytes 16777248 | tf_op jit(solution)/shard_map/all_to_all | solution.py:9
  283.9 8.8 %gather_fusion = bf16[256,64,128]{2,1,0:T(8,128)(2,1)} fusion(bf16[1024,64,128]{2,1,0:T(8,128)(2,1)} %bitcast.2, s32[1024]{0:T(1024)S(1)} %pad_clamp_fusion), kind=kCustom, calls=%fused_computation | custom fusion | bytes 8389632 | tf_op jit(solution)/shard_map/jit(_take)/gather | solution.py:32
  292.7 0.0 copy-start.2
  292.7 0.0 copy-start.1
  292.7 6.6 %fusion.7 = f32[32,64,128]{2,1,0:T(8,128)S(1)} fusion(bf16[32,1,8,128,128]{4,3,2,1,0:T(8,128)(2,1)} %param.8, bf16[32,8,64,128]{3,2,1,0:T(8,128)(2,1)} %bitcast.73, pred[32,8]{1,0:T(8,128)(4,1)S(1)} %copy.9), kind=kOutput, calls=%fused_computation.10 | convolution fusion | flops 538968064 | bytes 13631744 | tf_op jit(solution)/shard_map/jkrm,jkmn->jrn/dot_general | solution.py:34
  299.3 0.0 copy-done
  299.3 0.0 copy-done.2
  299.3 0.4 convolution_add_fusion
  299.8 2.9 collective-permute-start
  302.7 4.1 %collective-permute-done = f32[64,128]{1,0:T(8,128)S(1)} collective-permute-done((f32[64,128]{1,0:T(8,128)S(1)}, f32[64,128]{1,0:T(8,128)S(1)}, u32[]{:S(2)}, u32[]{:S(2)}) %collective-permute-start) | collective-permute-done | bytes 32800 | tf_op jit(solution)/shard_map/ppermute | solution.py:23
  306.8 0.0 copy-done.1
  306.8 0.2 convolution_add_fusion.6
  306.9 1.9 collective-permute-start.1
  308.9 5.1 %collective-permute-done.1 = f32[64,128]{1,0:T(8,128)S(1)} collective-permute-done((f32[64,128]{1,0:T(8,128)S(1)}, f32[64,128]{1,0:T(8,128)S(1)}, u32[]{:S(2)}, u32[]{:S(2)}) %collective-permute-start.1) | collective-permute-done | bytes 32800 | tf_op jit(solution)/shard_map/ppermute | solution.py:23
  314.0 0.2 convolution_add_fusion.5
  314.1 1.9 collective-permute-start.2
  316.1 5.1 %collective-permute-done.2 = f32[64,128]{1,0:T(8,128)S(1)} collective-permute-done((f32[64,128]{1,0:T(8,128)S(1)}, f32[64,128]{1,0:T(8,128)S(1)}, u32[]{:S(2)}, u32[]{:S(2)}) %collective-permute-start.2) | collective-permute-done | bytes 32800 | tf_op jit(solution)/shard_map/ppermute | solution.py:23
  321.2 0.2 convolution_add_fusion.4
  321.3 1.9 collective-permute-start.3
  323.3 5.1 %collective-permute-done.3 = f32[64,128]{1,0:T(8,128)S(1)} collective-permute-done((f32[64,128]{1,0:T(8,128)S(1)}, f32[64,128]{1,0:T(8,128)S(1)}, u32[]{:S(2)}, u32[]{:S(2)}) %collective-permute-start.3) | collective-permute-done | bytes 32800 | tf_op jit(solution)/shard_map/ppermute | solution.py:23
  328.3 0.2 convolution_add_fusion.3
  328.5 1.9 collective-permute-start.4
  330.4 5.4 %collective-permute-done.4 = f32[64,128]{1,0:T(8,128)S(1)} collective-permute-done((f32[64,128]{1,0:T(8,128)S(1)}, f32[64,128]{1,0:T(8,128)S(1)}, u32[]{:S(2)}, u32[]{:S(2)}) %collective-permute-start.4) | collective-permute-done | bytes 32800 | tf_op jit(solution)/shard_map/ppermute | solution.py:23
  335.9 0.2 convolution_add_fusion.2
  336.0 1.9 collective-permute-start.5
  338.0 5.1 %collective-permute-done.5 = f32[64,128]{1,0:T(8,128)S(1)} collective-permute-done((f32[64,128]{1,0:T(8,128)S(1)}, f32[64,128]{1,0:T(8,128)S(1)}, u32[]{:S(2)}, u32[]{:S(2)}) %collective-permute-start.5) | collective-permute-done | bytes 32800 | tf_op jit(solution)/shard_map/ppermute | solution.py:23
  343.1 0.2 convolution_add_fusion.1
  343.2 1.9 collective-permute-start.6
  345.2 5.1 %collective-permute-done.6 = f32[64,128]{1,0:T(8,128)S(1)} collective-permute-done((f32[64,128]{1,0:T(8,128)S(1)}, f32[64,128]{1,0:T(8,128)S(1)}, u32[]{:S(2)}, u32[]{:S(2)}) %collective-permute-start.6) | collective-permute-done | bytes 32800 | tf_op jit(solution)/shard_map/ppermute | solution.py:23
  350.3 1.5 fusion.6
  (4 shorter events, 0.0 us)
Async XLA Ops:
  0.0 299.3 %copy-start = (bf16[32,1,128,128]{3,2,1,0:T(8,128)(2,1)S(1)}, bf16[32,1,128,128]{3,2,1,0:T(8,128)(2,1)}, u32[]{:S(2)}) copy-start(bf16[32,1,128,128]{3,2,1,0:T(8,128)(2,1)} %param.9) | copy-start | bytes 3145732
  7.1 7.7 %copy-start.3 = (s32[32,1,8]{0,2,1:T(8,128)S(1)}, s32[32,1,8]{0,2,1:T(8,128)}, u32[]{:S(2)}) copy-start(s32[32,1,8]{0,2,1:T(8,128)} %param.11) | copy-start | bytes 3076
  7.1 276.7 %all-to-all-start = ((bf16[32,32,1,64,128]{4,3,2,1,0:T(8,128)(2,1)}), bf16[32,32,1,64,128]{4,3,2,1,0:T(8,128)(2,1)}, u32[]{:S(2)}, u32[]{:S(2)}) async-start(bf16[32,32,1,64,128]{4,3,2,1,0:T(8,128)(2,1)} %stack.2), calls=%async_computation | async-start | bytes 33554432 | tf_op jit(solution)/shard_map/all_to_all | solution.py:9
  292.7 6.6 %copy-start.2 = (bf16[32,1,64,128]{3,2,1,0:T(8,128)(2,1)S(1)}, bf16[32,1,64,128]{3,2,1,0:T(8,128)(2,1)}, u32[]{:S(2)}) copy-start(bf16[32,1,64,128]{3,2,1,0:T(8,128)(2,1)} %param.7) | copy-start | bytes 1572868
  292.7 14.1 %copy-start.1 = (bf16[32,1,128,128]{3,2,1,0:T(8,128)(2,1)S(1)}, bf16[32,1,128,128]{3,2,1,0:T(8,128)(2,1)}, u32[]{:S(2)}) copy-start(bf16[32,1,128,128]{3,2,1,0:T(8,128)(2,1)} %param.10) | copy-start | bytes 3145732
  299.8 7.0 %collective-permute-start = (f32[64,128]{1,0:T(8,128)S(1)}, f32[64,128]{1,0:T(8,128)S(1)}, u32[]{:S(2)}, u32[]{:S(2)}) collective-permute-start(f32[64,128]{1,0:T(8,128)S(1)} %slice_bitcast_fusion), channel_id=1, source_target_pairs={{0,1},{1,2},{2,3},{3,4},{4,5},{5,6},{6,7},{8,9},{9,10},{10,11},{11... | collective-permute-start | bytes 98312 | tf_op jit(solution)/shard_map/ppermute | solution.py:23
  306.9 7.0 %collective-permute-start.1 = (f32[64,128]{1,0:T(8,128)S(1)}, f32[64,128]{1,0:T(8,128)S(1)}, u32[]{:S(2)}, u32[]{:S(2)}) collective-permute-start(f32[64,128]{1,0:T(8,128)S(1)} %convolution_add_fusion.6), channel_id=1, source_target_pairs={{0,1},{1,2},{2,3},{3,4},{4,5},{5,6},{6,7},{8,9},{9,10},{10,11},{11... | collective-permute-start | bytes 98312 | tf_op jit(solution)/shard_map/ppermute | solution.py:23
  314.1 7.0 %collective-permute-start.2 = (f32[64,128]{1,0:T(8,128)S(1)}, f32[64,128]{1,0:T(8,128)S(1)}, u32[]{:S(2)}, u32[]{:S(2)}) collective-permute-start(f32[64,128]{1,0:T(8,128)S(1)} %convolution_add_fusion.5), channel_id=1, source_target_pairs={{0,1},{1,2},{2,3},{3,4},{4,5},{5,6},{6,7},{8,9},{9,10},{10,11},{11... | collective-permute-start | bytes 98312 | tf_op jit(solution)/shard_map/ppermute | solution.py:23
  321.3 7.0 %collective-permute-start.3 = (f32[64,128]{1,0:T(8,128)S(1)}, f32[64,128]{1,0:T(8,128)S(1)}, u32[]{:S(2)}, u32[]{:S(2)}) collective-permute-start(f32[64,128]{1,0:T(8,128)S(1)} %convolution_add_fusion.4), channel_id=1, source_target_pairs={{0,1},{1,2},{2,3},{3,4},{4,5},{5,6},{6,7},{8,9},{9,10},{10,11},{11... | collective-permute-start | bytes 98312 | tf_op jit(solution)/shard_map/ppermute | solution.py:23
  328.5 7.4 %collective-permute-start.4 = (f32[64,128]{1,0:T(8,128)S(1)}, f32[64,128]{1,0:T(8,128)S(1)}, u32[]{:S(2)}, u32[]{:S(2)}) collective-permute-start(f32[64,128]{1,0:T(8,128)S(1)} %convolution_add_fusion.3), channel_id=1, source_target_pairs={{0,1},{1,2},{2,3},{3,4},{4,5},{5,6},{6,7},{8,9},{9,10},{10,11},{11... | collective-permute-start | bytes 98312 | tf_op jit(solution)/shard_map/ppermute | solution.py:23
  336.0 7.0 %collective-permute-start.5 = (f32[64,128]{1,0:T(8,128)S(1)}, f32[64,128]{1,0:T(8,128)S(1)}, u32[]{:S(2)}, u32[]{:S(2)}) collective-permute-start(f32[64,128]{1,0:T(8,128)S(1)} %convolution_add_fusion.2), channel_id=1, source_target_pairs={{0,1},{1,2},{2,3},{3,4},{4,5},{5,6},{6,7},{8,9},{9,10},{10,11},{11... | collective-permute-start | bytes 98312 | tf_op jit(solution)/shard_map/ppermute | solution.py:23
  343.2 7.0 %collective-permute-start.6 = (f32[64,128]{1,0:T(8,128)S(1)}, f32[64,128]{1,0:T(8,128)S(1)}, u32[]{:S(2)}, u32[]{:S(2)}) collective-permute-start(f32[64,128]{1,0:T(8,128)S(1)} %convolution_add_fusion.1), channel_id=1, source_target_pairs={{0,1},{1,2},{2,3},{3,4},{4,5},{5,6},{6,7},{8,9},{9,10},{10,11},{11... | collective-permute-start | bytes 98312 | tf_op jit(solution)/shard_map/ppermute | solution.py:23
